TPU v7x, 256 devices: a whole 4x4x8 slice. The times are simulated.
256 devices in a mesh: band: 16 (over z, x_hi), fft: 16 (over x_lo, y, core).
Axes of the slice: x: 4 (x_hi: 2, x_lo: 2; x = x_hi * 2 + x_lo), y: 4, z: 8, core: 2. Of those that a mesh axis runs over, the one named last changes fastest.
Arguments:
- orbitals: bfloat16 [32, 128, 128, 128], P('band', 'fft'), may hold values from -6 to 6
- owner_order: int32 [2], replicated, may hold values from 0 to 15, as said below
- sphere_mask: int32 [128, 128, 128], P(None, 'fft'), may hold values from 0 to 1, as said below
Outputs:
- fock_images: float32 [32, 128, 128, 128], P('band', 'fft')
Inputs may be any that keep to these rules, and one draw needn't show every extreme that they name: `owner_order`: the 2 owner groups are all different, and group 16 - 1 owns one of the rounds. `sphere_mask`: zero wherever q of the steps is less than the square of 56.
All inputs are finite; a program needn't handle non-finite values.
Results may differ from a plain program's by a relative error of at most 0.018.
Values may be sent and summed in bfloat16 or wider, within the bound.
A program may use at most 64 MiB of HBM per device.

v0:
```python
import math
import jax
import jax.numpy as jnp
from jax import lax
from jax.sharding import PartitionSpec as P

ROUNDS = 2


def spread(block, axis, source):
    block = jnp.where(lax.axis_index(axis) == source, block, jnp.zeros_like(block))
    return lax.psum(block, axis)


def dft_tables(points):
    rows_index = lax.broadcasted_iota(jnp.int32, (points, points), 0)
    cols_index = lax.broadcasted_iota(jnp.int32, (points, points), 1)
    phases = 2.0 * math.pi / points * (rows_index * cols_index % points).astype(jnp.float32)
    cosine = jnp.cos(phases)
    sine = jnp.sin(phases)
    forward_x = jnp.concatenate(
        [jnp.concatenate([cosine, -sine], 1), jnp.concatenate([sine, cosine], 1)], 0
    )
    inverse_x = jnp.concatenate(
        [jnp.concatenate([cosine, sine], 1), jnp.concatenate([-sine, cosine], 1)], 0
    )
    stacked = jnp.concatenate([cosine, sine], 0)
    return (
        forward_x.astype(jnp.bfloat16),
        inverse_x.astype(jnp.bfloat16),
        stacked.astype(jnp.bfloat16),
    )


def coulomb_slab(sphere_mask):
    points = sphere_mask.shape[0]
    width = sphere_mask.shape[1]
    shape = sphere_mask.shape
    along_z = lax.broadcasted_iota(jnp.int32, shape, 0)
    along_y = lax.broadcasted_iota(jnp.int32, shape, 1) + lax.axis_index("fft") * width
    along_x = lax.broadcasted_iota(jnp.int32, shape, 2)

    def signed(values):
        return jnp.where(values < points // 2, values, values - points)

    freq_z, freq_y, freq_x = (signed(along_z), signed(along_y), signed(along_x))
    total_sq = freq_z * freq_z + freq_y * freq_y + freq_x * freq_x
    inverse = jnp.where(
        total_sq > 0, 1.0 / jnp.maximum(total_sq, 1).astype(jnp.float32), jnp.float32(0.0)
    )
    return sphere_mask.astype(jnp.float32) * inverse * jnp.float32(1.0 / (3.0 * float(points)))


def combine_parts(cos_part, sin_part, direction):
    halfway = cos_part.shape[-1] // 2
    real_part = cos_part[..., :halfway] + direction * sin_part[..., halfway:]
    imag_part = cos_part[..., halfway:] - direction * sin_part[..., :halfway]
    return jnp.concatenate([real_part, imag_part], axis=-1)


def along_rows(values_in, stacked, direction):
    points = stacked.shape[1]
    result = jnp.einsum("ay,fzyc->fzac", stacked, values_in, preferred_element_type=jnp.float32)
    return combine_parts(result[:, :, :points], result[:, :, points:], direction)


def along_columns(values_in, stacked, direction):
    points = stacked.shape[1]
    result = jnp.einsum("az,fzmc->famc", stacked, values_in, preferred_element_type=jnp.float32)
    return combine_parts(result[:, :points], result[:, points:], direction)


def respond_many(first_ones, second_ones, locals_in, tables, kernel, outward, return_trip):
    forward_x, inverse_x, stacked = tables
    points = kernel.shape[-1]
    count = locals_in.shape[0]
    packs = first_ones.shape[0]
    local_values = locals_in.astype(jnp.float32)[:, None]
    firsts = first_ones.astype(jnp.float32)[None]
    seconds = second_ones.astype(jnp.float32)[None]
    packed = jnp.concatenate(
        [
            (firsts * local_values).astype(jnp.bfloat16),
            (seconds * local_values).astype(jnp.bfloat16),
        ],
        axis=-1,
    )
    packed = packed.reshape((count * packs,) + packed.shape[2:])
    section_one = jnp.dot(packed, forward_x, preferred_element_type=jnp.float32).astype(
        jnp.bfloat16
    )
    section_two = along_rows(section_one, stacked, 1.0).astype(jnp.bfloat16)
    columns_data = outward(section_two)
    spectrum = along_columns(columns_data, stacked, 1.0)
    split_shape = spectrum.shape[:3] + (2, points)
    section_three = (
        (spectrum.reshape(split_shape) * kernel[:, :, None, :])
        .reshape(spectrum.shape)
        .astype(jnp.bfloat16)
    )
    section_four = along_columns(section_three, stacked, -1.0).astype(jnp.bfloat16)
    planes_data = return_trip(section_four)
    section_five = along_rows(planes_data, stacked, -1.0).astype(jnp.bfloat16)
    section_six = jnp.dot(section_five, inverse_x, preferred_element_type=jnp.float32)
    section_six = section_six.reshape((count, packs) + section_six.shape[1:])
    return -jnp.sum(
        firsts * section_six[..., :points] + seconds * section_six[..., points:], axis=1
    )


def shards(orbitals, owner_order, sphere_mask):
    points = orbitals.shape[-1]
    tables = dft_tables(points)
    kernel = coulomb_slab(sphere_mask)
    owner_list = []
    for round_index in range(ROUNDS):
        owner_list.append(spread(orbitals, "band", owner_order[round_index]))

    def outward(values_in):
        return lax.all_to_all(values_in, "fft", split_axis=2, concat_axis=1, tiled=True)

    def return_trip(values_in):
        return lax.all_to_all(values_in, "fft", split_axis=1, concat_axis=2, tiled=True)

    accumulated = jnp.zeros(orbitals.shape, jnp.float32)
    for round_index in range(ROUNDS):
        owner_rows = owner_list[round_index]
        first_ones = owner_rows[0::2]
        second_ones = owner_rows[1::2]

        def band_step(carry, local):
            return (
                carry,
                respond_many(
                    first_ones, second_ones, local[None], tables, kernel, outward, return_trip
                )[0],
            )

        unused, contributions = lax.scan(band_step, None, orbitals)
        accumulated = accumulated + contributions
    return accumulated


def solution(mesh):
    placed = (P("band", "fft", None, None), P(), P(None, "fft", None))
    return jax.shard_map(
        shards, mesh=mesh, in_specs=placed, out_specs=P("band", "fft", None, None), check_vma=False
    )
```

profile of v0, /device:TPU:1, one launch (start us, length us, event | category | flops | bytes accessed | tf_op | source)
XLA Modules:
  0.0 341.3 jit_solution(6651478727574558865)
XLA Ops:
  6.5 1.3 fusion.95
  9.1 2.1 broadcast_select_fusion
  13.2 152.5 %all-reduce.3.cloned.1.call-done = (bf16[2,8,128,128]{3,2,1,0:T(8,128)(2,1)}, bf16[2,8,128,128]{3,2,1,0:T(8,128)(2,1)}) async-done(((bf16[2,8,128,128]{3,2,1,0:T(8,128)(2,1)}, bf16[2,8,128,128]{3,2,1,0:T(8,128)(2,1)}), (bf16[2,8,128,128]{3,2,1,0:T(8,128)(2,1)}, bf16[2,8,128,128]{3,2,1,0:T(8,128)(2,1)})) %all-reduce.3.cloned.1.call-update) | async-done | bytes 1048592 | tf_op jit(solution)/shard_map/psum | solution.py:12
  165.7 1.3 fusion.93
  166.9 1.1 broadcast.64.clone.1
  168.0 87.5 %while.21 = (s32[]{:T(128)}, f32[2,8,128,128]{3,2,1,0:T(8,128)}, bf16[1,8,128,128]{3,2,1,0:T(8,128)(2,1)S(1)}, bf16[2,8,128,128]{3,2,1,0:T(8,128)(2,1)}, bf16[1,...) while((s32[]{:T(128)}, f32[2,8,128,128]{3,2,1,0:T(8,128)}, ...), condition=%wide.region_5.6_spmd, body=%wide.region_4.5_spmd.sunk | while | flops 814612480 | bytes 49021216 | solution.py:139
  168.0 2.0 fusion.159
  170.0 1.9 convolution_bitcast_fusion.25
  172.5 25.0 %all_to_all.57 = bf16[1,8,128,256]{3,1,0,2:T(8,128)(2,1)S(1)} all-to-all(bf16[1,8,128,256]{3,1,0,2:T(8,128)(2,1)S(1)} %copy.87), channel_id=1, replica_groups=mesh['band'=16,'fft'=16] {'fft'}, dimensions={2} | all-to-all | bytes 1048576 | tf_op jit(solution)/shard_map/while/body/eval_jaxpr/all_to_all | solution.py:120
  199.1 1.2 copy.90
  200.3 4.5 %all-to-all-start.3 = ((bf16[1,128,8,256]{3,2,0,1:T(8,128)(2,1)}), bf16[1,128,8,256]{3,2,0,1:T(8,128)(2,1)S(1)}, u32[]{:S(2)}, u32[]{:S(2)}) async-start(bf16[1,128,8,256]{3,2,0,1:T(8,128)(2,1)} %copy.90), calls=%async_computation.3 | async-start | bytes 1048576 | tf_op jit(solution)/shard_map/while/body/eval_jaxpr/all_to_all | solution.py:123
  204.8 9.9 %all-to-all-done.3 = bf16[1,128,8,256]{3,2,0,1:T(8,128)(2,1)S(1)} async-done(((bf16[1,128,8,256]{3,2,0,1:T(8,128)(2,1)}), bf16[1,128,8,256]{3,2,0,1:T(8,128)(2,1)S(1)}, u32[]{:S(2)}, u32[]{:S(2)}) %all-to-all-start.3) | async-done | bytes 524320 | tf_op jit(solution)/shard_map/while/body/eval_jaxpr/all_to_all | solution.py:123
  217.5 2.0 fusion.159
  219.5 1.9 convolution_bitcast_fusion.25
  222.0 13.5 %all_to_all.57 = bf16[1,8,128,256]{3,1,0,2:T(8,128)(2,1)S(1)} all-to-all(bf16[1,8,128,256]{3,1,0,2:T(8,128)(2,1)S(1)} %copy.87), channel_id=1, replica_groups=mesh['band'=16,'fft'=16] {'fft'}, dimensions={2} | all-to-all | bytes 1048576 | tf_op jit(solution)/shard_map/while/body/eval_jaxpr/all_to_all | solution.py:120
  237.0 1.2 copy.90
  238.2 4.5 %all-to-all-start.3 = ((bf16[1,128,8,256]{3,2,0,1:T(8,128)(2,1)}), bf16[1,128,8,256]{3,2,0,1:T(8,128)(2,1)S(1)}, u32[]{:S(2)}, u32[]{:S(2)}) async-start(bf16[1,128,8,256]{3,2,0,1:T(8,128)(2,1)} %copy.90), calls=%async_computation.3 | async-start | bytes 1048576 | tf_op jit(solution)/shard_map/while/body/eval_jaxpr/all_to_all | solution.py:123
  242.7 9.9 %all-to-all-done.3 = bf16[1,128,8,256]{3,2,0,1:T(8,128)(2,1)S(1)} async-done(((bf16[1,128,8,256]{3,2,0,1:T(8,128)(2,1)}), bf16[1,128,8,256]{3,2,0,1:T(8,128)(2,1)S(1)}, u32[]{:S(2)}, u32[]{:S(2)}) %all-to-all-start.3) | async-done | bytes 524320 | tf_op jit(solution)/shard_map/while/body/eval_jaxpr/all_to_all | solution.py:123
  256.6 75.2 %while.20 = (s32[]{:T(128)}, f32[2,8,128,128]{3,2,1,0:T(8,128)}, bf16[1,8,128,128]{3,2,1,0:T(8,128)(2,1)S(1)}, bf16[2,8,128,128]{3,2,1,0:T(8,128)(2,1)}, bf16[1,...) while((s32[]{:T(128)}, f32[2,8,128,128]{3,2,1,0:T(8,128)}, ...), condition=%wide.region_2.3_spmd, body=%wide.region_1.2_spmd.sunk | while | flops 814612480 | bytes 46924008 | solution.py:139
  256.6 1.8 fusion.142
  258.4 1.8 convolution_bitcast_fusion.20
  260.7 13.5 %all_to_all.56 = bf16[1,8,128,256]{3,1,0,2:T(8,128)(2,1)S(1)} all-to-all(bf16[1,8,128,256]{3,1,0,2:T(8,128)(2,1)S(1)} %copy.81), channel_id=1, replica_groups=mesh['band'=16,'fft'=16] {'fft'}, dimensions={2} | all-to-all | bytes 1048576 | tf_op jit(solution)/shard_map/while/body/eval_jaxpr/all_to_all | solution.py:120
  275.8 1.2 copy.84
  277.0 4.5 %all-to-all-start.1 = ((bf16[1,128,8,256]{3,2,0,1:T(8,128)(2,1)}), bf16[1,128,8,256]{3,2,0,1:T(8,128)(2,1)S(1)}, u32[]{:S(2)}, u32[]{:S(2)}) async-start(bf16[1,128,8,256]{3,2,0,1:T(8,128)(2,1)} %copy.84), calls=%async_computation.1 | async-start | bytes 1048576 | tf_op jit(solution)/shard_map/while/body/eval_jaxpr/all_to_all | solution.py:123
  281.5 9.9 %all-to-all-done.1 = bf16[1,128,8,256]{3,2,0,1:T(8,128)(2,1)S(1)} async-done(((bf16[1,128,8,256]{3,2,0,1:T(8,128)(2,1)}), bf16[1,128,8,256]{3,2,0,1:T(8,128)(2,1)S(1)}, u32[]{:S(2)}, u32[]{:S(2)}) %all-to-all-start.1) | async-done | bytes 524320 | tf_op jit(solution)/shard_map/while/body/eval_jaxpr/all_to_all | solution.py:123
  294.2 1.8 fusion.142
  296.0 1.8 convolution_bitcast_fusion.20
  298.3 13.5 %all_to_all.56 = bf16[1,8,128,256]{3,1,0,2:T(8,128)(2,1)S(1)} all-to-all(bf16[1,8,128,256]{3,1,0,2:T(8,128)(2,1)S(1)} %copy.81), channel_id=1, replica_groups=mesh['band'=16,'fft'=16] {'fft'}, dimensions={2} | all-to-all | bytes 1048576 | tf_op jit(solution)/shard_map/while/body/eval_jaxpr/all_to_all | solution.py:120
  313.4 1.2 copy.84
  314.6 4.5 %all-to-all-start.1 = ((bf16[1,128,8,256]{3,2,0,1:T(8,128)(2,1)}), bf16[1,128,8,256]{3,2,0,1:T(8,128)(2,1)S(1)}, u32[]{:S(2)}, u32[]{:S(2)}) async-start(bf16[1,128,8,256]{3,2,0,1:T(8,128)(2,1)} %copy.84), calls=%async_computation.1 | async-start | bytes 1048576 | tf_op jit(solution)/shard_map/while/body/eval_jaxpr/all_to_all | solution.py:123
  319.1 9.9 %all-to-all-done.1 = bf16[1,128,8,256]{3,2,0,1:T(8,128)(2,1)S(1)} async-done(((bf16[1,128,8,256]{3,2,0,1:T(8,128)(2,1)}), bf16[1,128,8,256]{3,2,0,1:T(8,128)(2,1)S(1)}, u32[]{:S(2)}, u32[]{:S(2)}) %all-to-all-start.1) | async-done | bytes 524320 | tf_op jit(solution)/shard_map/while/body/eval_jaxpr/all_to_all | solution.py:123
  331.8 2.6 add.91
  (107 shorter events, 22.4 us)
Async XLA Ops:
  6.5 4.7 %copy-start.8 = (s32[128,8,128]{2,1,0:T(8,128)S(1)}, s32[128,8,128]{2,1,0:T(8,128)}, u32[]{:S(2)}) copy-start(s32[128,8,128]{2,1,0:T(8,128)} %param.9) | copy-start | bytes 1572868
  6.5 159.1 %all-reduce.3.cloned.1.call-start = ((), (), s32[]{:S(2)}) async-start(), calls=%async_computation.4 | async-start | bytes 2097152 | tf_op jit(solution)/shard_map/psum | solution.py:12
  168.0 2.0 copy-start
  200.3 14.4 %all-to-all-start.3 = ((bf16[1,128,8,256]{3,2,0,1:T(8,128)(2,1)}), bf16[1,128,8,256]{3,2,0,1:T(8,128)(2,1)S(1)}, u32[]{:S(2)}, u32[]{:S(2)}) async-start(bf16[1,128,8,256]{3,2,0,1:T(8,128)(2,1)} %copy.90), calls=%async_computation.3 | async-start | bytes 1048576 | tf_op jit(solution)/shard_map/while/body/eval_jaxpr/all_to_all | solution.py:123
  214.7 0.9 copy-start.2
  215.1 1.0 copy-start.1
  215.1 1.3 copy-start.6
  216.6 1.0 copy-start.7
  217.5 2.0 copy-start
  238.2 14.4 %all-to-all-start.3 = ((bf16[1,128,8,256]{3,2,0,1:T(8,128)(2,1)}), bf16[1,128,8,256]{3,2,0,1:T(8,128)(2,1)S(1)}, u32[]{:S(2)}, u32[]{:S(2)}) async-start(bf16[1,128,8,256]{3,2,0,1:T(8,128)(2,1)} %copy.90), calls=%async_computation.3 | async-start | bytes 1048576 | tf_op jit(solution)/shard_map/while/body/eval_jaxpr/all_to_all | solution.py:123
  252.6 0.9 copy-start.2
  253.1 1.0 copy-start.1
  253.1 1.3 copy-start.6
  254.5 1.0 copy-start.7
  277.0 14.4 %all-to-all-start.1 = ((bf16[1,128,8,256]{3,2,0,1:T(8,128)(2,1)}), bf16[1,128,8,256]{3,2,0,1:T(8,128)(2,1)S(1)}, u32[]{:S(2)}, u32[]{:S(2)}) async-start(bf16[1,128,8,256]{3,2,0,1:T(8,128)(2,1)} %copy.84), calls=%async_computation.1 | async-start | bytes 1048576 | tf_op jit(solution)/shard_map/while/body/eval_jaxpr/all_to_all | solution.py:123
  291.4 0.9 copy-start.3
  291.9 1.2 copy-start.4
  293.2 1.0 copy-start.5
  314.6 14.4 %all-to-all-start.1 = ((bf16[1,128,8,256]{3,2,0,1:T(8,128)(2,1)}), bf16[1,128,8,256]{3,2,0,1:T(8,128)(2,1)S(1)}, u32[]{:S(2)}, u32[]{:S(2)}) async-start(bf16[1,128,8,256]{3,2,0,1:T(8,128)(2,1)} %copy.84), calls=%async_computation.1 | async-start | bytes 1048576 | tf_op jit(solution)/shard_map/while/body/eval_jaxpr/all_to_all | solution.py:123
  329.0 0.9 copy-start.3
  329.5 1.2 copy-start.4
  330.8 1.0 copy-start.5
Sparse Core Ops, SparseCore 0:
  11.4 154.2 all-reduce.2
where the time goes:
time: 342 us; the launch traced here: 341 us
  waiting for transfers between devices  192 us (56%)
  blocking collectives  65.5 us (19%)
  local copies, waits for them, and re-layouts  18.9 us (6%)
  starting transfers between devices  18.1 us (5%)
  other arithmetic  17.3 us (5%)
  between operations  14.8 us (4%)
  matrix products  14.2 us (4%)
    psum x1, waiting for transfers between devices, spread(): return lax.psum(block, axis)  153 us
    all_to_all x4, blocking collectives, outward(): lax.all_to_all(values_in, 'fft', split_axis=2, concat_axis=1, tiled=True)  65.5 us
    all_to_all x4, waiting for transfers between devices, return_trip(): lax.all_to_all(values_in, 'fft', split_axis=1, concat_axis=2, tiled=True)  39.5 us
    all_to_all x4, starting transfers between devices, return_trip(): lax.all_to_all(values_in, 'fft', split_axis=1, concat_axis=2, tiled=True)  18.1 us
    dot_general x8, matrix products, along_rows(): jnp.einsum('ay,fzyc->fzac', stacked, values_in, preferred_element_type=jn...  9.2 us
    convert_element_type x4, other arithmetic, respond_many(): (firsts * local_values).astype(jnp.bfloat16)  7.5 us
    while x32, local copies, waits for them, and re-layouts  6.97 us
  transfers between devices with their start and end apart: 5, of which 5 were waited for; matrix products, arithmetic and copies ran while one was open for 1% of the time, Pallas kernels for 0%

commit v1 on v0

--- a/solution.py
+++ b/solution.py
@@ -9,7 +9,12 @@
 
 def spread(block, axis, source):
     block = jnp.where(lax.axis_index(axis) == source, block, jnp.zeros_like(block))
-    return lax.psum(block, axis)
+
+    def pools_tell(shard_in, dev_axis):
+        arr_now = jnp.sum(lax.all_gather(shard_in, dev_axis), axis=0)
+        return arr_now
+
+    return pools_tell(block, axis)
 
 
 def dft_tables(points):

time: 342 us -> 457 us (1.34)
  waiting for transfers between devices: 192 us -> 307 us
  other arithmetic: 17.3 us -> 27.8 us
  blocking collectives: 65.5 us -> 55.4 us
    all_gather x0 -> x2, waiting for transfers between devices: none -> 267 us  [pools_tell(): arr_now = jnp.sum(lax.all_gather(shard_in, dev_axis), axis=0)]
    psum x1 -> x0, waiting for transfers between devices: 153 us -> none  [spread(): return lax.psum(block, axis)]
    reduce_sum x0 -> x2, other arithmetic: none -> 10.5 us  [pools_tell(): arr_now = jnp.sum(lax.all_gather(shard_in, dev_axis), axis=0)]
    all_to_all x4, blocking collectives: 65.5 us -> 55.4 us  [outward(): lax.all_to_all(values_in, 'fft', split_axis=2, concat_axis=1, tiled=True)]
  transfers between devices with their start and end apart: 5 -> 6, of which waited for: 5 -> 6; matrix products, arithmetic and copies ran while one was open for 1% -> 2% of each run, Pallas kernels for 0% -> 0%
where the time goes in v1:
time: 457 us; the launch traced here: 455 us
  waiting for transfers between devices  307 us (67%)
  blocking collectives  55.4 us (12%)
  other arithmetic  27.8 us (6%)
  starting transfers between devices  18.1 us (4%)
  local copies, waits for them, and re-layouts  17.8 us (4%)
  between operations  14.7 us (3%)
  matrix products  14.2 us (3%)
    all_gather x2, waiting for transfers between devices, pools_tell(): arr_now = jnp.sum(lax.all_gather(shard_in, dev_axis), axis=0)  267 us
    all_to_all x4, blocking collectives, outward(): lax.all_to_all(values_in, 'fft', split_axis=2, concat_axis=1, tiled=True)  55.4 us
    all_to_all x4, waiting for transfers between devices, return_trip(): lax.all_to_all(values_in, 'fft', split_axis=1, concat_axis=2, tiled=True)  39.5 us
    all_to_all x4, starting transfers between devices, return_trip(): lax.all_to_all(values_in, 'fft', split_axis=1, concat_axis=2, tiled=True)  18.1 us
    reduce_sum x2, other arithmetic, pools_tell(): arr_now = jnp.sum(lax.all_gather(shard_in, dev_axis), axis=0)  10.5 us
    dot_general x8, matrix products, along_rows(): jnp.einsum('ay,fzyc->fzac', stacked, values_in, preferred_element_type=jn...  9.21 us
  transfers between devices with their start and end apart: 6, of which 6 were waited for; matrix products, arithmetic and copies ran while one was open for 2% of the time, Pallas kernels for 0%

profile of v1, /device:TPU:1, one launch (start us, length us, event | category | flops | bytes accessed | tf_op | source)
XLA Modules:
  0.0 455.5 jit_solution(11976078944982327982)
XLA Ops:
  6.5 1.3 fusion.95
  9.1 2.1 broadcast_select_fusion
  13.8 136.7 %all-gather.7.cloned.1.call-done = bf16[32,8,128,128]{3,2,1,0:T(8,128)(2,1)} async-done(((bf16[2,8,128,128]{3,2,1,0:T(8,128)(2,1)}), bf16[32,8,128,128]{3,2,1,0:T(8,128)(2,1)}) %all-gather.7.cloned.1.call-update) | async-done | bytes 8388624 | tf_op jit(solution)/shard_map/all_gather | solution.py:14
  150.6 5.3 %reduce_sum.33 = bf16[2,8,128,128]{3,2,1,0:T(8,128)(2,1)S(1)} reduce(bf16[16,2,8,128,128]{4,3,2,1,0:T(8,128)(2,1)} %bitcast.264, bf16[]{:T(256)} %constant.62.clone.1), dimensions={0}, to_apply=%region_3.4 | reduce | flops 3932160 | bytes 8912898 | tf_op jit(solution)/shard_map/reduce_sum | solution.py:14
  155.9 130.0 %all-gather.5.cloned.1.call-done = bf16[32,8,128,128]{3,2,1,0:T(8,128)(2,1)} async-done(((bf16[2,8,128,128]{3,2,1,0:T(8,128)(2,1)}), bf16[32,8,128,128]{3,2,1,0:T(8,128)(2,1)}) %all-gather.5.cloned.1.call-update) | async-done | bytes 8388624 | tf_op jit(solution)/shard_map/all_gather | solution.py:14
  285.8 5.3 %reduce_sum.32 = bf16[2,8,128,128]{3,2,1,0:T(8,128)(2,1)S(1)} reduce(bf16[16,2,8,128,128]{4,3,2,1,0:T(8,128)(2,1)} %bitcast.265, bf16[]{:T(256)} %constant.62.clone.1), dimensions={0}, to_apply=%region_0.1 | reduce | flops 3932160 | bytes 8912898 | tf_op jit(solution)/shard_map/reduce_sum | solution.py:14
  292.2 77.5 %while.20 = (s32[]{:T(128)}, f32[2,8,128,128]{3,2,1,0:T(8,128)}, bf16[1,8,128,128]{3,2,1,0:T(8,128)(2,1)S(1)}, bf16[2,8,128,128]{3,2,1,0:T(8,128)(2,1)}, bf16[1,...) while((s32[]{:T(128)}, f32[2,8,128,128]{3,2,1,0:T(8,128)}, ...), condition=%wide.region_2.3_spmd, body=%wide.region_1.2_spmd.sunk | while | flops 814612480 | bytes 49021216 | solution.py:144
  292.2 2.0 fusion.142
  294.2 1.9 convolution_bitcast_fusion.20
  296.7 15.0 %all_to_all.56 = bf16[1,8,128,256]{3,1,0,2:T(8,128)(2,1)S(1)} all-to-all(bf16[1,8,128,256]{3,1,0,2:T(8,128)(2,1)S(1)} %copy.81), channel_id=1, replica_groups=mesh['band'=16,'fft'=16] {'fft'}, dimensions={2} | all-to-all | bytes 1048576 | tf_op jit(solution)/shard_map/while/body/eval_jaxpr/all_to_all | solution.py:125
  313.2 1.2 copy.84
  314.4 4.5 all-to-all-start.1
  318.9 9.9 %all-to-all-done.1 = bf16[1,128,8,256]{3,2,0,1:T(8,128)(2,1)S(1)} async-done(((bf16[1,128,8,256]{3,2,0,1:T(8,128)(2,1)}), bf16[1,128,8,256]{3,2,0,1:T(8,128)(2,1)S(1)}, u32[]{:S(2)}, u32[]{:S(2)}) %all-to-all-start.1) | async-done | bytes 524320 | tf_op jit(solution)/shard_map/while/body/eval_jaxpr/all_to_all | solution.py:128
  331.7 2.0 fusion.142
  333.7 1.9 convolution_bitcast_fusion.20
  336.1 13.5 %all_to_all.56 = bf16[1,8,128,256]{3,1,0,2:T(8,128)(2,1)S(1)} all-to-all(bf16[1,8,128,256]{3,1,0,2:T(8,128)(2,1)S(1)} %copy.81), channel_id=1, replica_groups=mesh['band'=16,'fft'=16] {'fft'}, dimensions={2} | all-to-all | bytes 1048576 | tf_op jit(solution)/shard_map/while/body/eval_jaxpr/all_to_all | solution.py:125
  351.2 1.2 copy.84
  352.4 4.5 all-to-all-start.1
  356.9 9.9 %all-to-all-done.1 = bf16[1,128,8,256]{3,2,0,1:T(8,128)(2,1)S(1)} async-done(((bf16[1,128,8,256]{3,2,0,1:T(8,128)(2,1)}), bf16[1,128,8,256]{3,2,0,1:T(8,128)(2,1)S(1)}, u32[]{:S(2)}, u32[]{:S(2)}) %all-to-all-start.1) | async-done | bytes 524320 | tf_op jit(solution)/shard_map/while/body/eval_jaxpr/all_to_all | solution.py:128
  370.8 75.2 %while.21 = (s32[]{:T(128)}, f32[2,8,128,128]{3,2,1,0:T(8,128)}, bf16[1,8,128,128]{3,2,1,0:T(8,128)(2,1)S(1)}, bf16[2,8,128,128]{3,2,1,0:T(8,128)(2,1)}, bf16[1,...) while((s32[]{:T(128)}, f32[2,8,128,128]{3,2,1,0:T(8,128)}, ...), condition=%wide.region_5.6_spmd, body=%wide.region_4.5_spmd.sunk | while | flops 814612480 | bytes 46924008 | solution.py:144
  370.8 1.8 fusion.159
  372.6 1.8 convolution_bitcast_fusion.25
  374.9 13.5 %all_to_all.57 = bf16[1,8,128,256]{3,1,0,2:T(8,128)(2,1)S(1)} all-to-all(bf16[1,8,128,256]{3,1,0,2:T(8,128)(2,1)S(1)} %copy.87), channel_id=1, replica_groups=mesh['band'=16,'fft'=16] {'fft'}, dimensions={2} | all-to-all | bytes 1048576 | tf_op jit(solution)/shard_map/while/body/eval_jaxpr/all_to_all | solution.py:125
  390.0 1.2 copy.90
  391.2 4.5 all-to-all-start.3
  395.7 9.9 %all-to-all-done.3 = bf16[1,128,8,256]{3,2,0,1:T(8,128)(2,1)S(1)} async-done(((bf16[1,128,8,256]{3,2,0,1:T(8,128)(2,1)}), bf16[1,128,8,256]{3,2,0,1:T(8,128)(2,1)S(1)}, u32[]{:S(2)}, u32[]{:S(2)}) %all-to-all-start.3) | async-done | bytes 524320 | tf_op jit(solution)/shard_map/while/body/eval_jaxpr/all_to_all | solution.py:128
  408.4 1.8 fusion.159
  410.2 1.8 convolution_bitcast_fusion.25
  412.6 13.5 %all_to_all.57 = bf16[1,8,128,256]{3,1,0,2:T(8,128)(2,1)S(1)} all-to-all(bf16[1,8,128,256]{3,1,0,2:T(8,128)(2,1)S(1)} %copy.87), channel_id=1, replica_groups=mesh['band'=16,'fft'=16] {'fft'}, dimensions={2} | all-to-all | bytes 1048576 | tf_op jit(solution)/shard_map/while/body/eval_jaxpr/all_to_all | solution.py:125
  428.8 4.5 all-to-all-start.3
  433.3 9.9 %all-to-all-done.3 = bf16[1,128,8,256]{3,2,0,1:T(8,128)(2,1)S(1)} async-done(((bf16[1,128,8,256]{3,2,0,1:T(8,128)(2,1)}), bf16[1,128,8,256]{3,2,0,1:T(8,128)(2,1)S(1)}, u32[]{:S(2)}, u32[]{:S(2)}) %all-to-all-start.3) | async-done | bytes 524320 | tf_op jit(solution)/shard_map/while/body/eval_jaxpr/all_to_all | solution.py:128
  446.0 2.6 add.87
  (113 shorter events, 25.5 us)
Async XLA Ops:
  6.5 5.4 %copy-start.8 = (s32[128,8,128]{2,1,0:T(8,128)S(1)}, s32[128,8,128]{2,1,0:T(8,128)}, u32[]{:S(2)}) copy-start(s32[128,8,128]{2,1,0:T(8,128)} %param.9) | copy-start | bytes 1572868
  6.5 144.0 %all-gather.7.cloned.1.call-start = ((), (), s32[]{:S(2)}) async-start(), calls=%async_computation.5 | async-start | bytes 8912896 | tf_op jit(solution)/shard_map/all_gather | solution.py:14
  11.2 274.6 %all-gather.5.cloned.1.call-start = ((), (), s32[]{:S(2)}) async-start(), calls=%async_computation.4 | async-start | bytes 8912896 | tf_op jit(solution)/shard_map/all_gather | solution.py:14
  292.2 2.0 copy-start
  314.4 14.4 %all-to-all-start.1 = ((bf16[1,128,8,256]{3,2,0,1:T(8,128)(2,1)}), bf16[1,128,8,256]{3,2,0,1:T(8,128)(2,1)S(1)}, u32[]{:S(2)}, u32[]{:S(2)}) async-start(bf16[1,128,8,256]{3,2,0,1:T(8,128)(2,1)} %copy.84), calls=%async_computation.1 | async-start | bytes 1048576 | tf_op jit(solution)/shard_map/while/body/eval_jaxpr/all_to_all | solution.py:128
  328.8 0.9 copy-start.2
  329.3 1.0 copy-start.1
  329.3 1.3 copy-start.6
  330.7 1.0 copy-start.7
  331.7 2.0 copy-start
  352.4 14.4 %all-to-all-start.1 = ((bf16[1,128,8,256]{3,2,0,1:T(8,128)(2,1)}), bf16[1,128,8,256]{3,2,0,1:T(8,128)(2,1)S(1)}, u32[]{:S(2)}, u32[]{:S(2)}) async-start(bf16[1,128,8,256]{3,2,0,1:T(8,128)(2,1)} %copy.84), calls=%async_computation.1 | async-start | bytes 1048576 | tf_op jit(solution)/shard_map/while/body/eval_jaxpr/all_to_all | solution.py:128
  366.8 0.9 copy-start.2
  367.3 1.0 copy-start.1
  367.3 1.3 copy-start.6
  368.7 1.0 copy-start.7
  391.2 14.4 %all-to-all-start.3 = ((bf16[1,128,8,256]{3,2,0,1:T(8,128)(2,1)}), bf16[1,128,8,256]{3,2,0,1:T(8,128)(2,1)S(1)}, u32[]{:S(2)}, u32[]{:S(2)}) async-start(bf16[1,128,8,256]{3,2,0,1:T(8,128)(2,1)} %copy.90), calls=%async_computation.3 | async-start | bytes 1048576 | tf_op jit(solution)/shard_map/while/body/eval_jaxpr/all_to_all | solution.py:128
  405.6 0.9 copy-start.3
  406.1 1.2 copy-start.4
  407.4 1.0 copy-start.5
  428.8 14.4 %all-to-all-start.3 = ((bf16[1,128,8,256]{3,2,0,1:T(8,128)(2,1)}), bf16[1,128,8,256]{3,2,0,1:T(8,128)(2,1)S(1)}, u32[]{:S(2)}, u32[]{:S(2)}) async-start(bf16[1,128,8,256]{3,2,0,1:T(8,128)(2,1)} %copy.90), calls=%async_computation.3 | async-start | bytes 1048576 | tf_op jit(solution)/shard_map/while/body/eval_jaxpr/all_to_all | solution.py:128
  443.2 0.9 copy-start.3
  443.7 1.2 copy-start.4
  445.0 1.0 copy-start.5
Sparse Core Ops, SparseCore 0:
  11.3 139.1 all-gather.6
  153.1 132.6 all-gather.4
